TPU v7x, 512 devices: a whole 4x8x8 slice. The times are simulated.
512 devices in a mesh: brick: 64 (over z, y), blk: 8 (over x, core).
Axes of the slice: x: 4, y: 8, z: 8, core: 2. Of those that a mesh axis runs over, the one named last changes fastest.
Arguments:
- parameters: float32 [4, 65536], P(None, ('brick', 'blk')), may hold values from -0.4 to 3, as said below
- sersic: float32 [65536], P(('brick', 'blk')), may hold values from 1 to 4
- psf_width: float32 [65536], P(('brick', 'blk')), may hold values from 0.8 to 2
- point_flag: int32 [65536], P(('brick', 'blk')), may hold values 0 or 1
- owner_brick: int32 [65536, 1], P(('brick', 'blk')), may hold values from 0 to 63; in each aligned block of 128 rows (0 to 127, 128 to 255, ...) at most 4 rows name the same one
- cell_index: int32 [65536], P(('brick', 'blk')), may hold values from 0 to 31
- exposure: float32 [16384, 1024], P(('brick', 'blk')), may hold values from -120 to 120
- inv_noise: float32 [16384], P(('brick', 'blk')), may hold values from 0.5 to 2
Outputs:
- updated: float32 [4, 65536], P(None, ('brick', 'blk'))
Inputs may be any that keep to these rules, and one draw needn't show every extreme that they name: `parameters`: row 0 is a flux from 0.5 to 3, rows 1 and 2 the centre's offsets within 0.4 pixels, row 3 the log radius from ln 1.5 to ln 6. `owner_brick`: the sources of one device name one brick at most 4 times.
All inputs are finite; a program needn't handle non-finite values. No bound on the sum of `point_flag` on one device may be relied on, other than what follows from the above.
Results may differ from a plain program's by a relative error of at most 0.0003.
Values sent between devices are 32-bit elements; how exact they have to be, the bound alone decides.
A program may use at most 64 MiB of HBM per device.

v0:
```python
import math
import jax
import jax.numpy as jnp
from jax import lax
from jax.sharding import PartitionSpec as P

TILE = 32
series_terms = 96
zero_point = 30.0
base_damping = 0.1
misfit_scale = 0.05
block_rows = 32
highest = lax.Precision.HIGHEST


def incomplete_gamma(shape_value, cutoff):
    term_steps = jnp.arange(1, series_terms, dtype=cutoff.dtype)
    increments = jnp.log(cutoff)[None, :] - jnp.log(shape_value[None, :] + term_steps[:, None])
    partial_logs = jnp.concatenate(
        [jnp.zeros_like(cutoff)[None, :], jnp.cumsum(increments, axis=0)], axis=0
    )
    prefactor = shape_value * jnp.log(cutoff) - cutoff - lax.lgamma(shape_value + 1.0)
    return jnp.sum(jnp.exp(prefactor[None, :] + partial_logs), axis=0)


def render(values, sersic, psf_width, point_flag):
    flux_value = values[0]
    shift_x = values[1]
    shift_y = values[2]
    log_radius = values[3]
    coords = jnp.arange(TILE, dtype=values.dtype) + 0.5 - 0.5 * TILE
    offset_y = coords[None, :] - shift_y[:, None]
    offset_x = coords[None, :] - shift_x[:, None]
    radius_sq = offset_y[:, :, None] ** 2 + offset_x[:, None, :] ** 2
    inverse_index = 1.0 / sersic
    bfactor = 2.0 * sersic - 1.0 / 3.0 + 4.0 / (405.0 * sersic)
    cutoff = bfactor * jnp.exp((math.log(0.5 * TILE) - log_radius) * inverse_index)
    log_norm = (
        jnp.log(2.0 * math.pi * sersic)
        + 2.0 * log_radius
        + lax.lgamma(2.0 * sersic)
        - 2.0 * sersic * jnp.log(bfactor)
        + jnp.log(incomplete_gamma(2.0 * sersic, cutoff))
    )
    scaled = jnp.exp(
        (0.5 * jnp.log(radius_sq) - log_radius[:, None, None]) * inverse_index[:, None, None]
    )
    galaxy = jnp.exp(-bfactor[:, None, None] * scaled - log_norm[:, None, None])
    separation = coords[:, None] - coords[None, :]
    inv_two_var = 0.5 / (psf_width * psf_width)
    norm_psf = 1.0 / (math.sqrt(2.0 * math.pi) * psf_width)
    kernel = jnp.exp(-(separation**2)[None] * inv_two_var[:, None, None]) * norm_psf[:, None, None]
    blurred = jnp.einsum("bij,bjk->bik", kernel, galaxy, precision=highest)
    blurred = jnp.einsum("bik,blk->bil", blurred, kernel, precision=highest)
    profile_y = jnp.exp(-(offset_y**2) * inv_two_var[:, None]) * norm_psf[:, None]
    profile_x = jnp.exp(-(offset_x**2) * inv_two_var[:, None]) * norm_psf[:, None]
    point_image = profile_y[:, :, None] * profile_x[:, None, :]
    shape_image = jnp.where((point_flag == 1)[:, None, None], point_image, blurred)
    return (zero_point * flux_value)[:, None] * shape_image.reshape(values.shape[1], TILE * TILE)


def source_moments(values, sersic, psf_width, point_flag, weighted_rows, weight_rows):

    def model_of(current):
        return render(current, sersic, psf_width, point_flag)

    unit_tangents = jnp.eye(4, dtype=values.dtype)[:, :, None] * jnp.ones_like(values)[None]
    jacobian = jax.vmap(lambda tangent: jax.jvp(model_of, (values,), (tangent,))[1])(unit_tangents)
    gradient = jnp.einsum("pbq,bq->pb", jacobian, weighted_rows, precision=highest)
    curvature = (
        jnp.einsum("pbq,rbq->prb", jacobian, jacobian, precision=highest)
        * weight_rows[None, None, :]
    )
    return (gradient, curvature)


def damped_solve(curvature, gradient, damping):
    system = [[curvature[first, second] for second in range(4)] for first in range(4)]
    for first in range(4):
        system[first][first] = system[first][first] + damping * (1.0 + curvature[first, first])
    factor = [[None for second in range(4)] for first in range(4)]
    for column in range(4):
        pivot = system[column][column]
        for inner in range(column):
            pivot = pivot - factor[column][inner] * factor[column][inner]
        pivot = jnp.sqrt(pivot)
        factor[column][column] = pivot
        for lower_row in range(column + 1, 4):
            entry = system[lower_row][column]
            for inner in range(column):
                entry = entry - factor[lower_row][inner] * factor[column][inner]
            factor[lower_row][column] = entry / pivot
    forward = []
    for row_at in range(4):
        entry = gradient[row_at]
        for inner in range(row_at):
            entry = entry - factor[row_at][inner] * forward[inner]
        forward.append(entry / factor[row_at][row_at])
    solution = [None, None, None, None]
    for row_at in reversed(range(4)):
        entry = forward[row_at]
        for inner in range(row_at + 1, 4):
            entry = entry - factor[inner][row_at] * solution[inner]
        solution[row_at] = entry / factor[row_at][row_at]
    return jnp.stack(solution)


def rendered_tiles(values, sersic, psf_width, point_flag):
    count = values.shape[1]
    groups = count // block_rows
    stacked = (
        values.reshape(4, groups, block_rows).transpose(1, 0, 2),
        sersic.reshape(groups, block_rows),
        psf_width.reshape(groups, block_rows),
        point_flag.reshape(groups, block_rows),
    )
    tiles = lax.map(lambda block: render(block[0], block[1], block[2], block[3]), stacked)
    return tiles.reshape(count, TILE * TILE)


def blocked_moments(values, sersic, psf_width, point_flag, weighted_rows, weight_rows):
    count = values.shape[1]
    groups = count // block_rows
    stacked = (
        values.reshape(4, groups, block_rows).transpose(1, 0, 2),
        sersic.reshape(groups, block_rows),
        psf_width.reshape(groups, block_rows),
        point_flag.reshape(groups, block_rows),
        weighted_rows.reshape(groups, block_rows, TILE * TILE),
        weight_rows.reshape(groups, block_rows),
    )
    gradient, curvature = lax.map(
        lambda block: source_moments(block[0], block[1], block[2], block[3], block[4], block[5]),
        stacked,
    )
    gradient = gradient.transpose(1, 0, 2).reshape(4, count)
    curvature = curvature.transpose(1, 2, 0, 3).reshape(4, 4, count)
    return (gradient, curvature)


def cell_residuals(exposure, weights, slot_cells, slot_tiles):
    cell_ids = jnp.arange(exposure.shape[0], dtype=jnp.int32)
    selector = (cell_ids[:, None] == slot_cells[None, :]).astype(exposure.dtype)
    model = jnp.dot(selector, slot_tiles, precision=highest)
    misfit = exposure - model
    weighted = weights[:, None] * misfit
    local_chi = jnp.sum(weighted * misfit)
    slot_rows = jnp.dot(selector.T, weighted, precision=highest)
    slot_weights = jnp.dot(selector.T, weights, precision=highest)
    return (local_chi, slot_rows, slot_weights)


def shards(parameters, sersic, psf_width, point_flag, owner_brick, cell_index, exposure, inv_noise):
    source_count = parameters.shape[1]
    bricks = lax.axis_size("brick")
    slot_count = 2 * source_count
    capacity = slot_count // bricks
    destination = owner_brick[:, 0]
    matches = (destination[:, None] == jnp.arange(bricks, dtype=jnp.int32)[None, :]).astype(
        jnp.int32
    )
    earlier = jnp.cumsum(matches, axis=0) - matches
    rank_within = jnp.sum(earlier * matches, axis=1)
    slot_of = destination * capacity + rank_within
    weights = inv_noise * inv_noise
    pixel_total = lax.axis_size("blk") * exposure.shape[0] * exposure.shape[1]
    tiles = rendered_tiles(parameters, sersic, psf_width, point_flag)
    outgoing = jnp.zeros((slot_count, tiles.shape[1]), tiles.dtype).at[slot_of].set(tiles)
    outgoing_cells = jnp.full((slot_count,), -1, jnp.int32).at[slot_of].set(cell_index)
    incoming, incoming_cells = (
        lax.all_to_all(outgoing, "brick", split_axis=0, concat_axis=0, tiled=True),
        lax.all_to_all(outgoing_cells, "brick", split_axis=0, concat_axis=0, tiled=True),
    )
    local_chi, slot_rows, slot_weights = cell_residuals(exposure, weights, incoming_cells, incoming)
    returned, returned_weights = (
        lax.all_to_all(slot_rows, "brick", split_axis=0, concat_axis=0, tiled=True),
        lax.all_to_all(slot_weights, "brick", split_axis=0, concat_axis=0, tiled=True),
    )
    gradient, curvature = blocked_moments(
        parameters, sersic, psf_width, point_flag, returned[slot_of], returned_weights[slot_of]
    )
    group_chi = lax.psum(local_chi, "blk")
    damping = base_damping + misfit_scale * group_chi / pixel_total
    return parameters + damped_solve(curvature, gradient, damping)


def solution(mesh):
    in_specs = (
        P(None, ("brick", "blk")),
        P(("brick", "blk")),
        P(("brick", "blk")),
        P(("brick", "blk")),
        P(("brick", "blk"), None),
        P(("brick", "blk")),
        P(("brick", "blk"), None),
        P(("brick", "blk")),
    )
    out_specs = P(None, ("brick", "blk"))
    return jax.shard_map(shards, mesh=mesh, in_specs=in_specs, out_specs=out_specs, check_vma=False)
```

profile of v0, /device:TPU:6, one launch (start us, length us, event | category | flops | bytes accessed | tf_op | source)
XLA Modules:
  0.0 205.0 jit_solution(13674835427051204987)
XLA Ops:
  4.2 16.6 %all-to-all-start = ((s32[64,4,1]{1,2,0:T(1,128)}), s32[64,4,1]{1,2,0:T(1,128)S(1)}, u32[]{:S(2)}, u32[]{:S(2)}) async-start(s32[64,4,1]{1,2,0:T(1,128)} %bitcast.49), calls=%async_computation | async-start | bytes 65536 | tf_op jit(solution)/shard_map/all_to_all | solution.py:172
  24.4 14.8 %while.32 = (s32[]{:T(128)}, f32[4,32,1024]{2,1,0:T(8,128)S(1)}, f32[4,4,32]{2,1,0:T(4,128)S(1)}, s32[4,32]{1,0:T(4,128)}, f32[4,32]{1,0:T(4,128)S(1)}, /*index=5*/f32[4,32]{1,0:T(4,128)S(1)}, s32[]{:T(128)}, f32[]{:T(128)}) while((s32[]{:T(128)}, f32[4,32,1024]{2,1,0:T(8,128)S(1)}, f32[4,4,32]{2,1,0:T(4,128)S(1)}, s32[4,32]{1,0:T(4,128)}, ...), condition=%wide.region_6.7_spmd, body=%wide.region_3.6_spmd.sunk | while | flops 25907552 | bytes 1019813 | solution.py:117
  41.8 12.8 %all-to-all-start.1 = ((f32[64,4,1024]{2,1,0:T(4,128)}), f32[64,4,1024]{2,1,0:T(4,128)S(1)}, u32[]{:S(2)}, u32[]{:S(2)}) async-start(f32[64,4,1024]{2,1,0:T(4,128)} %all_to_all.32), calls=%async_computation.1 | async-start | bytes 2097152 | tf_op jit(solution)/shard_map/all_to_all | solution.py:171
  57.1 26.7 %all-to-all-done.1 = f32[64,4,1024]{2,1,0:T(4,128)S(1)} async-done(((f32[64,4,1024]{2,1,0:T(4,128)}), f32[64,4,1024]{2,1,0:T(4,128)S(1)}, u32[]{:S(2)}, u32[]{:S(2)}) %all-to-all-start.1) | async-done | bytes 1048608 | tf_op jit(solution)/shard_map/all_to_all | solution.py:171
  83.8 6.5 %all-to-all-start.3 = ((f32[64,4,1]{1,2,0:T(1,128)}), f32[64,4,1]{1,2,0:T(1,128)S(1)}, u32[]{:S(2)}, u32[]{:S(2)}) async-start(f32[64,4,1]{1,2,0:T(1,128)} %bitcast.55), calls=%async_computation.3 | async-start | bytes 65536 | tf_op jit(solution)/shard_map/all_to_all | solution.py:177
  93.8 8.6 %all-to-all-done.3 = f32[64,4,1]{1,2,0:T(1,128)S(1)} async-done(((f32[64,4,1]{1,2,0:T(1,128)}), f32[64,4,1]{1,2,0:T(1,128)S(1)}, u32[]{:S(2)}, u32[]{:S(2)}) %all-to-all-start.3) | async-done | bytes 1056 | tf_op jit(solution)/shard_map/all_to_all | solution.py:177
  102.3 4.7 %all-to-all-start.2 = ((f32[64,4,1024]{2,1,0:T(4,128)}), f32[64,4,1024]{2,1,0:T(4,128)S(1)}, u32[]{:S(2)}, u32[]{:S(2)}) async-start(f32[64,4,1024]{2,1,0:T(4,128)} %all_to_all.35), calls=%async_computation.2 | async-start | bytes 2097152 | tf_op jit(solution)/shard_map/all_to_all | solution.py:176
  109.6 11.2 %psum.7 = f32[]{:T(128)} all-reduce(f32[]{:T(128)} %get-tuple-element.534), channel_id=1, replica_groups=mesh['brick'=64,'blk'=8] {'blk'}, use_global_device_ids=true, to_apply=%region_15.16 | all-reduce | flops 1 | bytes 8 | tf_op jit(solution)/shard_map/psum | solution.py:182
  121.4 13.4 %all-to-all-done.2 = f32[64,4,1024]{2,1,0:T(4,128)S(1)} async-done(((f32[64,4,1024]{2,1,0:T(4,128)}), f32[64,4,1024]{2,1,0:T(4,128)S(1)}, u32[]{:S(2)}, u32[]{:S(2)}) %all-to-all-start.2) | async-done | bytes 1048608 | tf_op jit(solution)/shard_map/all_to_all | solution.py:176
  135.9 65.0 %while.33 = (s32[]{:T(128)}, f32[4,4,32]{2,1,0:T(4,128)}, f32[4,4,4,32]{1,2,3,0:T(4,128)S(1)}, f32[4,32,1024]{2,1,0:T(8,128)S(1)}, s32[4,32]{1,0:T(4,128)}, /*in...) while((s32[]{:T(128)}, f32[4,4,32]{2,1,0:T(4,128)}, ...), condition=%wide.region_13.14_spmd, body=%wide.region_8.13_spmd.sunk | while | flops 138444880 | bytes 6357045 | solution.py:132
  137.9 2.9 %fusion.184 = f32[32,32,4,32]{3,1,2,0:T(8,128)S(1)} fusion(f32[32,32,32]{2,1,0:T(8,128)S(1)} %get-tuple-element.723, f32[4,32]{0,1:T(8,128)S(1)} %copy.83, f32[32,32,32]{2,1,0:T(8,128)S(1)} %get-tuple-element.731, f32[32]{0:T(128)S(1)} %bitcast.320, f32[4]{0:T(128)S(1)} %get-tuple-element.732, f32[32,32,32]{2,1,0:T(8,128)S(1)} %get-tuple-element.733, ...), kind=kOutput, calls=%fused_computation.100.clone.1 | convolution fusion | flops 51576832 | bytes 955408 | tf_op jit(solution)/shard_map/while/body/eval_jaxpr/vmap(jvp(bij,bjk->bik))/dot_general | solution.py:53
  141.5 2.2 %bitcast_select_fusion.2 = f32[4,32,32,32]{3,2,0,1:T(8,128)S(1)} fusion(f32[32,32,4,32]{3,1,2,0:T(8,128)S(1)} %fusion.184, f32[4,32,32]{2,0,1:T(4,128)S(1)} %get-tuple-element.743, f32[32,32]{1,0:T(8,128)S(1)} %get-tuple-element.744, f32[32,32]{1,0:T(8,128)S(1)} %get-tuple-element.745, f32[4,32,32]{2,0,1:T(4,128)S(1)} %get-tuple-element.746, ...), kind=kOutput, calls=%fused_computation.99.clone.1 | convolution fusion | flops 50921472 | bytes 1093920 | tf_op jit(solution)/shard_map/while/body/eval_jaxpr/vmap(jvp(bik,blk->bil))/dot_general | solution.py:54
  147.1 2.3 %fusion.187 = f32[4,4,4,32]{1,2,3,0:T(4,128)S(1)} fusion(f32[4,4,4,32]{1,2,3,0:T(4,128)S(1)} %get-tuple-element.787, s32[]{:T(128)} %get-tuple-element.785, f32[4,32,1024]{2,0,1:T(4,128)S(1)} %reshape.2358, f32[32]{0:T(128)S(1)} %get-tuple-element.747, f32[32,1024]{1,0:T(8,128)S(1)} %mul.2955, f32[4]{0:T(128)S(1)} %get-tuple-element.748, ...), kind=kOutput, calls=%fused_computation.113.clone.1 | convolution fusion | flops 6685184 | bytes 722436 | tf_op jit(solution)/shard_map/while/body/eval_jaxpr/pbq,rbq->prb/dot_general | solution.py:71
  149.4 2.2 %fusion.186 = f32[32,1,4]{2,1,0:T(1,128)S(1)} fusion(f32[4,32,1024]{2,0,1:T(4,128)S(1)} %reshape.2358, f32[32]{0:T(128)S(1)} %get-tuple-element.747, f32[32,1024]{1,0:T(8,128)S(1)} %mul.2955, f32[4]{0:T(128)S(1)} %get-tuple-element.748, f32[32,1024,1]{1,0,2:T(8,128)S(1)} %dynamic-slice_bitcast_fusion.2), kind=kOutput, calls=%fused_computation.131.clone.1 | convolution fusion | flops 1966080 | bytes 787088 | tf_op jit(solution)/shard_map/while/body/eval_jaxpr/pbq,bq->pb/dot_general | solution.py:69
  154.1 2.9 %fusion.184 = f32[32,32,4,32]{3,1,2,0:T(8,128)S(1)} fusion(f32[32,32,32]{2,1,0:T(8,128)S(1)} %get-tuple-element.723, f32[4,32]{0,1:T(8,128)S(1)} %copy.83, f32[32,32,32]{2,1,0:T(8,128)S(1)} %get-tuple-element.731, f32[32]{0:T(128)S(1)} %bitcast.320, f32[4]{0:T(128)S(1)} %get-tuple-element.732, f32[32,32,32]{2,1,0:T(8,128)S(1)} %get-tuple-element.733, ...), kind=kOutput, calls=%fused_computation.100.clone.1 | convolution fusion | flops 51576832 | bytes 955408 | tf_op jit(solution)/shard_map/while/body/eval_jaxpr/vmap(jvp(bij,bjk->bik))/dot_general | solution.py:53
  157.7 2.2 %bitcast_select_fusion.2 = f32[4,32,32,32]{3,2,0,1:T(8,128)S(1)} fusion(f32[32,32,4,32]{3,1,2,0:T(8,128)S(1)} %fusion.184, f32[4,32,32]{2,0,1:T(4,128)S(1)} %get-tuple-element.743, f32[32,32]{1,0:T(8,128)S(1)} %get-tuple-element.744, f32[32,32]{1,0:T(8,128)S(1)} %get-tuple-element.745, f32[4,32,32]{2,0,1:T(4,128)S(1)} %get-tuple-element.746, ...), kind=kOutput, calls=%fused_computation.99.clone.1 | convolution fusion | flops 50921472 | bytes 1093920 | tf_op jit(solution)/shard_map/while/body/eval_jaxpr/vmap(jvp(bik,blk->bil))/dot_general | solution.py:54
  163.3 2.3 %fusion.187 = f32[4,4,4,32]{1,2,3,0:T(4,128)S(1)} fusion(f32[4,4,4,32]{1,2,3,0:T(4,128)S(1)} %get-tuple-element.787, s32[]{:T(128)} %get-tuple-element.785, f32[4,32,1024]{2,0,1:T(4,128)S(1)} %reshape.2358, f32[32]{0:T(128)S(1)} %get-tuple-element.747, f32[32,1024]{1,0:T(8,128)S(1)} %mul.2955, f32[4]{0:T(128)S(1)} %get-tuple-element.748, ...), kind=kOutput, calls=%fused_computation.113.clone.1 | convolution fusion | flops 6685184 | bytes 722436 | tf_op jit(solution)/shard_map/while/body/eval_jaxpr/pbq,rbq->prb/dot_general | solution.py:71
  165.6 2.2 %fusion.186 = f32[32,1,4]{2,1,0:T(1,128)S(1)} fusion(f32[4,32,1024]{2,0,1:T(4,128)S(1)} %reshape.2358, f32[32]{0:T(128)S(1)} %get-tuple-element.747, f32[32,1024]{1,0:T(8,128)S(1)} %mul.2955, f32[4]{0:T(128)S(1)} %get-tuple-element.748, f32[32,1024,1]{1,0,2:T(8,128)S(1)} %dynamic-slice_bitcast_fusion.2), kind=kOutput, calls=%fused_computation.131.clone.1 | convolution fusion | flops 1966080 | bytes 787088 | tf_op jit(solution)/shard_map/while/body/eval_jaxpr/pbq,bq->pb/dot_general | solution.py:69
  170.3 2.9 %fusion.184 = f32[32,32,4,32]{3,1,2,0:T(8,128)S(1)} fusion(f32[32,32,32]{2,1,0:T(8,128)S(1)} %get-tuple-element.723, f32[4,32]{0,1:T(8,128)S(1)} %copy.83, f32[32,32,32]{2,1,0:T(8,128)S(1)} %get-tuple-element.731, f32[32]{0:T(128)S(1)} %bitcast.320, f32[4]{0:T(128)S(1)} %get-tuple-element.732, f32[32,32,32]{2,1,0:T(8,128)S(1)} %get-tuple-element.733, ...), kind=kOutput, calls=%fused_computation.100.clone.1 | convolution fusion | flops 51576832 | bytes 955408 | tf_op jit(solution)/shard_map/while/body/eval_jaxpr/vmap(jvp(bij,bjk->bik))/dot_general | solution.py:53
  173.9 2.2 %bitcast_select_fusion.2 = f32[4,32,32,32]{3,2,0,1:T(8,128)S(1)} fusion(f32[32,32,4,32]{3,1,2,0:T(8,128)S(1)} %fusion.184, f32[4,32,32]{2,0,1:T(4,128)S(1)} %get-tuple-element.743, f32[32,32]{1,0:T(8,128)S(1)} %get-tuple-element.744, f32[32,32]{1,0:T(8,128)S(1)} %get-tuple-element.745, f32[4,32,32]{2,0,1:T(4,128)S(1)} %get-tuple-element.746, ...), kind=kOutput, calls=%fused_computation.99.clone.1 | convolution fusion | flops 50921472 | bytes 1093920 | tf_op jit(solution)/shard_map/while/body/eval_jaxpr/vmap(jvp(bik,blk->bil))/dot_general | solution.py:54
  179.4 2.3 %fusion.187 = f32[4,4,4,32]{1,2,3,0:T(4,128)S(1)} fusion(f32[4,4,4,32]{1,2,3,0:T(4,128)S(1)} %get-tuple-element.787, s32[]{:T(128)} %get-tuple-element.785, f32[4,32,1024]{2,0,1:T(4,128)S(1)} %reshape.2358, f32[32]{0:T(128)S(1)} %get-tuple-element.747, f32[32,1024]{1,0:T(8,128)S(1)} %mul.2955, f32[4]{0:T(128)S(1)} %get-tuple-element.748, ...), kind=kOutput, calls=%fused_computation.113.clone.1 | convolution fusion | flops 6685184 | bytes 722436 | tf_op jit(solution)/shard_map/while/body/eval_jaxpr/pbq,rbq->prb/dot_general | solution.py:71
  186.5 2.9 %fusion.184 = f32[32,32,4,32]{3,1,2,0:T(8,128)S(1)} fusion(f32[32,32,32]{2,1,0:T(8,128)S(1)} %get-tuple-element.723, f32[4,32]{0,1:T(8,128)S(1)} %copy.83, f32[32,32,32]{2,1,0:T(8,128)S(1)} %get-tuple-element.731, f32[32]{0:T(128)S(1)} %bitcast.320, f32[4]{0:T(128)S(1)} %get-tuple-element.732, f32[32,32,32]{2,1,0:T(8,128)S(1)} %get-tuple-element.733, ...), kind=kOutput, calls=%fused_computation.100.clone.1 | convolution fusion | flops 51576832 | bytes 955408 | tf_op jit(solution)/shard_map/while/body/eval_jaxpr/vmap(jvp(bij,bjk->bik))/dot_general | solution.py:53
  190.1 2.2 %bitcast_select_fusion.2 = f32[4,32,32,32]{3,2,0,1:T(8,128)S(1)} fusion(f32[32,32,4,32]{3,1,2,0:T(8,128)S(1)} %fusion.184, f32[4,32,32]{2,0,1:T(4,128)S(1)} %get-tuple-element.743, f32[32,32]{1,0:T(8,128)S(1)} %get-tuple-element.744, f32[32,32]{1,0:T(8,128)S(1)} %get-tuple-element.745, f32[4,32,32]{2,0,1:T(4,128)S(1)} %get-tuple-element.746, ...), kind=kOutput, calls=%fused_computation.99.clone.1 | convolution fusion | flops 50921472 | bytes 1093920 | tf_op jit(solution)/shard_map/while/body/eval_jaxpr/vmap(jvp(bik,blk->bil))/dot_general | solution.py:54
  195.7 2.3 %fusion.187 = f32[4,4,4,32]{1,2,3,0:T(4,128)S(1)} fusion(f32[4,4,4,32]{1,2,3,0:T(4,128)S(1)} %get-tuple-element.787, s32[]{:T(128)} %get-tuple-element.785, f32[4,32,1024]{2,0,1:T(4,128)S(1)} %reshape.2358, f32[32]{0:T(128)S(1)} %get-tuple-element.747, f32[32,1024]{1,0:T(8,128)S(1)} %mul.2955, f32[4]{0:T(128)S(1)} %get-tuple-element.748, ...), kind=kOutput, calls=%fused_computation.113.clone.1 | convolution fusion | flops 6685184 | bytes 722436 | tf_op jit(solution)/shard_map/while/body/eval_jaxpr/pbq,rbq->prb/dot_general | solution.py:71
  (267 shorter events, 68.0 us)
Async XLA Ops:
  4.2 37.6 %all-to-all-start = ((s32[64,4,1]{1,2,0:T(1,128)}), s32[64,4,1]{1,2,0:T(1,128)S(1)}, u32[]{:S(2)}, u32[]{:S(2)}) async-start(s32[64,4,1]{1,2,0:T(1,128)} %bitcast.49), calls=%async_computation | async-start | bytes 65536 | tf_op jit(solution)/shard_map/all_to_all | solution.py:172
  40.5 14.2 %copy-start.2 = (f32[32]{0:T(128)S(1)}, f32[32]{0:T(128)}, u32[]{:S(2)}) copy-start(f32[32]{0:T(128)} %param.19) | copy-start | bytes 388
  41.8 48.8 %copy-start = (f32[32,1024]{1,0:T(8,128)S(1)}, f32[32,1024]{1,0:T(8,128)}, u32[]{:S(2)}) copy-start(f32[32,1024]{1,0:T(8,128)} %param.18) | copy-start | bytes 393220
  41.8 42.0 %all-to-all-start.1 = ((f32[64,4,1024]{2,1,0:T(4,128)}), f32[64,4,1024]{2,1,0:T(4,128)S(1)}, u32[]{:S(2)}, u32[]{:S(2)}) async-start(f32[64,4,1024]{2,1,0:T(4,128)} %all_to_all.32), calls=%async_computation.1 | async-start | bytes 2097152 | tf_op jit(solution)/shard_map/all_to_all | solution.py:171
  83.8 18.5 %all-to-all-start.3 = ((f32[64,4,1]{1,2,0:T(1,128)}), f32[64,4,1]{1,2,0:T(1,128)S(1)}, u32[]{:S(2)}, u32[]{:S(2)}) async-start(f32[64,4,1]{1,2,0:T(1,128)} %bitcast.55), calls=%async_computation.3 | async-start | bytes 65536 | tf_op jit(solution)/shard_map/all_to_all | solution.py:177
  102.3 32.5 %all-to-all-start.2 = ((f32[64,4,1024]{2,1,0:T(4,128)}), f32[64,4,1024]{2,1,0:T(4,128)S(1)}, u32[]{:S(2)}, u32[]{:S(2)}) async-start(f32[64,4,1024]{2,1,0:T(4,128)} %all_to_all.35), calls=%async_computation.2 | async-start | bytes 2097152 | tf_op jit(solution)/shard_map/all_to_all | solution.py:176
  135.9 68.4 %copy-start.1 = (f32[4,128]{1,0:T(4,128)S(1)}, f32[4,128]{1,0:T(4,128)}, u32[]{:S(2)}) copy-start(f32[4,128]{1,0:T(4,128)} %param.12) | copy-start | bytes 6148
where the time goes:
time: 206 us; the launch traced here: 205 us
  matrix products  57.5 us (28%)
  waiting for transfers between devices  48.6 us (24%)
  starting transfers between devices  40.5 us (20%)
  local copies, waits for them, and re-layouts  26.4 us (13%)
  other arithmetic  18.7 us (9%)
  blocking collectives  11.2 us (5%)
    all_to_all x1, waiting for transfers between devices, shards(): lax.all_to_all(outgoing, 'brick', split_axis=0, concat_axis=0, tiled=True)  26.7 us
    dot_general x12, matrix products, render(): blurred = jnp.einsum('bij,bjk->bik', kernel, galaxy, precision=highest)  19.7 us
    dot_general x12, matrix products, render(): blurred = jnp.einsum('bik,blk->bil', blurred, kernel, precision=highest)  17.4 us
    all_to_all x1, starting transfers between devices, shards(): lax.all_to_all(outgoing_cells, 'brick', split_axis=0, concat_axis=0, tile...  16.6 us
    all_to_all x1, waiting for transfers between devices, shards(): lax.all_to_all(slot_rows, 'brick', split_axis=0, concat_axis=0, tiled=True)  13.4 us
    all_to_all x1, starting transfers between devices, shards(): lax.all_to_all(outgoing, 'brick', split_axis=0, concat_axis=0, tiled=True)  12.8 us
    psum x1, blocking collectives, shards(): group_chi = lax.psum(local_chi, 'blk')  11.2 us
    dot_general x4, matrix products, source_moments(): jnp.einsum('pbq,rbq->prb', jacobian, jacobian, precision=highest)  9.38 us
  transfers between devices with their start and end apart: 4, of which 3 were waited for; matrix products, arithmetic and copies ran while one was open for 12% of the time, Pallas kernels for 0%

commit v1 on v0

--- a/solution.py
+++ b/solution.py
@@ -179,7 +179,11 @@
     gradient, curvature = blocked_moments(
         parameters, sersic, psf_width, point_flag, returned[slot_of], returned_weights[slot_of]
     )
-    group_chi = lax.psum(local_chi, "blk")
+    group_chi = local_chi
+    for hop in (1, 2, 4):
+        group_chi = group_chi + lax.ppermute(
+            group_chi, "blk", [(dev, dev ^ hop) for dev in range(8)]
+        )
     damping = base_damping + misfit_scale * group_chi / pixel_total
     return parameters + damped_solve(curvature, gradient, damping)
 

time: 206 us -> 206 us (level)
  blocking collectives: 11.2 us -> 0 us
  starting transfers between devices: 40.5 us -> 51 us
    psum x1 -> x0, blocking collectives: 11.2 us -> none  [shards(): group_chi = lax.psum(local_chi, 'blk')]
    ppermute x0 -> x3, starting transfers between devices: none -> 10.5 us  [shards(): lax.ppermute(group_chi, 'blk', [(dev, dev ^ hop) for dev in range(8)])]
    all_to_all x1, waiting for transfers between devices: 13.4 us -> 7.09 us  [shards(): lax.all_to_all(slot_rows, 'brick', split_axis=0, concat_axis=0, tiled=True)]
    ppermute x0 -> x3, waiting for transfers between devices: none -> 5.04 us  [shards(): lax.ppermute(group_chi, 'blk', [(dev, dev ^ hop) for dev in range(8)])]
  transfers between devices with their start and end apart: 4 -> 7, of which waited for: 3 -> 6; matrix products, arithmetic and copies ran while one was open for 12% -> 12% of each run, Pallas kernels for 0% -> 0%
where the time goes in v1:
time: 206 us; the launch traced here: 205 us
  matrix products  57.5 us (28%)
  starting transfers between devices  51 us (25%)
  waiting for transfers between devices  47.4 us (23%)
  local copies, waits for them, and re-layouts  26.4 us (13%)
  other arithmetic  18.7 us (9%)
  between operations  2.73 us (1%)
    all_to_all x1, waiting for transfers between devices, shards(): lax.all_to_all(outgoing, 'brick', split_axis=0, concat_axis=0, tiled=True)  26.7 us
    dot_general x12, matrix products, render(): blurred = jnp.einsum('bij,bjk->bik', kernel, galaxy, precision=highest)  19.7 us
    dot_general x12, matrix products, render(): blurred = jnp.einsum('bik,blk->bil', blurred, kernel, precision=highest)  17.4 us
    all_to_all x1, starting transfers between devices, shards(): lax.all_to_all(outgoing_cells, 'brick', split_axis=0, concat_axis=0, tile...  16.6 us
    all_to_all x1, starting transfers between devices, shards(): lax.all_to_all(outgoing, 'brick', split_axis=0, concat_axis=0, tiled=True)  12.8 us
    ppermute x3, starting transfers between devices, shards(): lax.ppermute(group_chi, 'blk', [(dev, dev ^ hop) for dev in range(8)])  10.5 us
    dot_general x4, matrix products, source_moments(): jnp.einsum('pbq,rbq->prb', jacobian, jacobian, precision=highest)  9.38 us
    dot_general x4, matrix products, source_moments(): jnp.einsum('pbq,bq->pb', jacobian, weighted_rows, precision=highest)  8.96 us
  transfers between devices with their start and end apart: 7, of which 6 were waited for; matrix products, arithmetic and copies ran while one was open for 12% of the time, Pallas kernels for 0%

profile of v1, /device:TPU:6, one launch (start us, length us, event | category | flops | bytes accessed | tf_op | source)
XLA Modules:
  0.0 205.0 jit_solution(6794515072890308651)
XLA Ops:
  4.2 16.6 %all-to-all-start = ((s32[64,4,1]{1,2,0:T(1,128)}), s32[64,4,1]{1,2,0:T(1,128)S(1)}, u32[]{:S(2)}, u32[]{:S(2)}) async-start(s32[64,4,1]{1,2,0:T(1,128)} %bitcast.49), calls=%async_computation | async-start | bytes 65536 | tf_op jit(solution)/shard_map/all_to_all | solution.py:172
  24.4 14.8 %while.32 = (s32[]{:T(128)}, f32[4,32,1024]{2,1,0:T(8,128)S(1)}, f32[4,4,32]{2,1,0:T(4,128)S(1)}, s32[4,32]{1,0:T(4,128)}, f32[4,32]{1,0:T(4,128)S(1)}, /*index=5*/f32[4,32]{1,0:T(4,128)S(1)}, s32[]{:T(128)}, f32[]{:T(128)}) while((s32[]{:T(128)}, f32[4,32,1024]{2,1,0:T(8,128)S(1)}, f32[4,4,32]{2,1,0:T(4,128)S(1)}, s32[4,32]{1,0:T(4,128)}, ...), condition=%wide.region_6.7_spmd, body=%wide.region_3.6_spmd.sunk | while | flops 25907552 | bytes 1019813 | solution.py:117
  41.8 12.8 %all-to-all-start.1 = ((f32[64,4,1024]{2,1,0:T(4,128)}), f32[64,4,1024]{2,1,0:T(4,128)S(1)}, u32[]{:S(2)}, u32[]{:S(2)}) async-start(f32[64,4,1024]{2,1,0:T(4,128)} %all_to_all.32), calls=%async_computation.1 | async-start | bytes 2097152 | tf_op jit(solution)/shard_map/all_to_all | solution.py:171
  57.1 26.7 %all-to-all-done.1 = f32[64,4,1024]{2,1,0:T(4,128)S(1)} async-done(((f32[64,4,1024]{2,1,0:T(4,128)}), f32[64,4,1024]{2,1,0:T(4,128)S(1)}, u32[]{:S(2)}, u32[]{:S(2)}) %all-to-all-start.1) | async-done | bytes 1048608 | tf_op jit(solution)/shard_map/all_to_all | solution.py:171
  83.8 6.5 %all-to-all-start.3 = ((f32[64,4,1]{1,2,0:T(1,128)}), f32[64,4,1]{1,2,0:T(1,128)S(1)}, u32[]{:S(2)}, u32[]{:S(2)}) async-start(f32[64,4,1]{1,2,0:T(1,128)} %bitcast.55), calls=%async_computation.3 | async-start | bytes 65536 | tf_op jit(solution)/shard_map/all_to_all | solution.py:177
  93.8 8.6 %all-to-all-done.3 = f32[64,4,1]{1,2,0:T(1,128)S(1)} async-done(((f32[64,4,1]{1,2,0:T(1,128)}), f32[64,4,1]{1,2,0:T(1,128)S(1)}, u32[]{:S(2)}, u32[]{:S(2)}) %all-to-all-start.3) | async-done | bytes 1056 | tf_op jit(solution)/shard_map/all_to_all | solution.py:177
  102.3 4.7 %all-to-all-start.2 = ((f32[64,4,1024]{2,1,0:T(4,128)}), f32[64,4,1024]{2,1,0:T(4,128)S(1)}, u32[]{:S(2)}, u32[]{:S(2)}) async-start(f32[64,4,1024]{2,1,0:T(4,128)} %all_to_all.35), calls=%async_computation.2 | async-start | bytes 2097152 | tf_op jit(solution)/shard_map/all_to_all | solution.py:176
  114.1 4.0 %collective-permute-start.1 = (f32[]{:T(128)}, f32[]{:T(128)}, u32[]{:S(2)}, u32[]{:S(2)}) collective-permute-start(f32[]{:T(128)} %add.943), channel_id=1, source_target_pairs={{0,2},{1,3},{2,0},{3,1},{4,6},{5,7},{6,4},{7,5},{8,10},{9,11},{10,... | collective-permute-start | bytes 20 | tf_op jit(solution)/shard_map/ppermute | solution.py:184
  120.1 4.6 %collective-permute-start.2 = (f32[]{:T(128)}, f32[]{:T(128)}, u32[]{:S(2)}, u32[]{:S(2)}) collective-permute-start(f32[]{:T(128)} %add.944), channel_id=1, source_target_pairs={{0,4},{1,5},{2,6},{3,7},{4,0},{5,1},{6,2},{7,3},{8,12},{9,13},{10,... | collective-permute-start | bytes 20 | tf_op jit(solution)/shard_map/ppermute | solution.py:184
  124.7 2.3 %collective-permute-done.2 = f32[]{:T(128)} collective-permute-done((f32[]{:T(128)}, f32[]{:T(128)}, u32[]{:S(2)}, u32[]{:S(2)}) %collective-permute-start.2) | collective-permute-done | bytes 36 | tf_op jit(solution)/shard_map/ppermute | solution.py:184
  127.7 7.1 %all-to-all-done.2 = f32[64,4,1024]{2,1,0:T(4,128)S(1)} async-done(((f32[64,4,1024]{2,1,0:T(4,128)}), f32[64,4,1024]{2,1,0:T(4,128)S(1)}, u32[]{:S(2)}, u32[]{:S(2)}) %all-to-all-start.2) | async-done | bytes 1048608 | tf_op jit(solution)/shard_map/all_to_all | solution.py:176
  135.9 65.0 %while.33 = (s32[]{:T(128)}, f32[4,4,32]{2,1,0:T(4,128)}, f32[4,4,4,32]{1,2,3,0:T(4,128)S(1)}, f32[4,32,1024]{2,1,0:T(8,128)S(1)}, s32[4,32]{1,0:T(4,128)}, /*in...) while((s32[]{:T(128)}, f32[4,4,32]{2,1,0:T(4,128)}, ...), condition=%wide.region_13.14_spmd, body=%wide.region_8.13_spmd.sunk | while | flops 138444880 | bytes 6357045 | solution.py:132
  137.9 2.9 %fusion.184 = f32[32,32,4,32]{3,1,2,0:T(8,128)S(1)} fusion(f32[32,32,32]{2,1,0:T(8,128)S(1)} %get-tuple-element.723, f32[4,32]{0,1:T(8,128)S(1)} %copy.83, f32[32,32,32]{2,1,0:T(8,128)S(1)} %get-tuple-element.731, f32[32]{0:T(128)S(1)} %bitcast.320, f32[4]{0:T(128)S(1)} %get-tuple-element.732, f32[32,32,32]{2,1,0:T(8,128)S(1)} %get-tuple-element.733, ...), kind=kOutput, calls=%fused_computation.100.clone.1 | convolution fusion | flops 51576832 | bytes 955408 | tf_op jit(solution)/shard_map/while/body/eval_jaxpr/vmap(jvp(bij,bjk->bik))/dot_general | solution.py:53
  141.5 2.2 %bitcast_select_fusion.2 = f32[4,32,32,32]{3,2,0,1:T(8,128)S(1)} fusion(f32[32,32,4,32]{3,1,2,0:T(8,128)S(1)} %fusion.184, f32[4,32,32]{2,0,1:T(4,128)S(1)} %get-tuple-element.743, f32[32,32]{1,0:T(8,128)S(1)} %get-tuple-element.744, f32[32,32]{1,0:T(8,128)S(1)} %get-tuple-element.745, f32[4,32,32]{2,0,1:T(4,128)S(1)} %get-tuple-element.746, ...), kind=kOutput, calls=%fused_computation.99.clone.1 | convolution fusion | flops 50921472 | bytes 1093920 | tf_op jit(solution)/shard_map/while/body/eval_jaxpr/vmap(jvp(bik,blk->bil))/dot_general | solution.py:54
  147.1 2.3 %fusion.187 = f32[4,4,4,32]{1,2,3,0:T(4,128)S(1)} fusion(f32[4,4,4,32]{1,2,3,0:T(4,128)S(1)} %get-tuple-element.787, s32[]{:T(128)} %get-tuple-element.785, f32[4,32,1024]{2,0,1:T(4,128)S(1)} %reshape.2358, f32[32]{0:T(128)S(1)} %get-tuple-element.747, f32[32,1024]{1,0:T(8,128)S(1)} %mul.2955, f32[4]{0:T(128)S(1)} %get-tuple-element.748, ...), kind=kOutput, calls=%fused_computation.113.clone.1 | convolution fusion | flops 6685184 | bytes 722436 | tf_op jit(solution)/shard_map/while/body/eval_jaxpr/pbq,rbq->prb/dot_general | solution.py:71
  154.1 2.9 %fusion.184 = f32[32,32,4,32]{3,1,2,0:T(8,128)S(1)} fusion(f32[32,32,32]{2,1,0:T(8,128)S(1)} %get-tuple-element.723, f32[4,32]{0,1:T(8,128)S(1)} %copy.83, f32[32,32,32]{2,1,0:T(8,128)S(1)} %get-tuple-element.731, f32[32]{0:T(128)S(1)} %bitcast.320, f32[4]{0:T(128)S(1)} %get-tuple-element.732, f32[32,32,32]{2,1,0:T(8,128)S(1)} %get-tuple-element.733, ...), kind=kOutput, calls=%fused_computation.100.clone.1 | convolution fusion | flops 51576832 | bytes 955408 | tf_op jit(solution)/shard_map/while/body/eval_jaxpr/vmap(jvp(bij,bjk->bik))/dot_general | solution.py:53
  157.7 2.2 %bitcast_select_fusion.2 = f32[4,32,32,32]{3,2,0,1:T(8,128)S(1)} fusion(f32[32,32,4,32]{3,1,2,0:T(8,128)S(1)} %fusion.184, f32[4,32,32]{2,0,1:T(4,128)S(1)} %get-tuple-element.743, f32[32,32]{1,0:T(8,128)S(1)} %get-tuple-element.744, f32[32,32]{1,0:T(8,128)S(1)} %get-tuple-element.745, f32[4,32,32]{2,0,1:T(4,128)S(1)} %get-tuple-element.746, ...), kind=kOutput, calls=%fused_computation.99.clone.1 | convolution fusion | flops 50921472 | bytes 1093920 | tf_op jit(solution)/shard_map/while/body/eval_jaxpr/vmap(jvp(bik,blk->bil))/dot_general | solution.py:54
  163.3 2.3 %fusion.187 = f32[4,4,4,32]{1,2,3,0:T(4,128)S(1)} fusion(f32[4,4,4,32]{1,2,3,0:T(4,128)S(1)} %get-tuple-element.787, s32[]{:T(128)} %get-tuple-element.785, f32[4,32,1024]{2,0,1:T(4,128)S(1)} %reshape.2358, f32[32]{0:T(128)S(1)} %get-tuple-element.747, f32[32,1024]{1,0:T(8,128)S(1)} %mul.2955, f32[4]{0:T(128)S(1)} %get-tuple-element.748, ...), kind=kOutput, calls=%fused_computation.113.clone.1 | convolution fusion | flops 6685184 | bytes 722436 | tf_op jit(solution)/shard_map/while/body/eval_jaxpr/pbq,rbq->prb/dot_general | solution.py:71
  170.3 2.9 %fusion.184 = f32[32,32,4,32]{3,1,2,0:T(8,128)S(1)} fusion(f32[32,32,32]{2,1,0:T(8,128)S(1)} %get-tuple-element.723, f32[4,32]{0,1:T(8,128)S(1)} %copy.83, f32[32,32,32]{2,1,0:T(8,128)S(1)} %get-tuple-element.731, f32[32]{0:T(128)S(1)} %bitcast.320, f32[4]{0:T(128)S(1)} %get-tuple-element.732, f32[32,32,32]{2,1,0:T(8,128)S(1)} %get-tuple-element.733, ...), kind=kOutput, calls=%fused_computation.100.clone.1 | convolution fusion | flops 51576832 | bytes 955408 | tf_op jit(solution)/shard_map/while/body/eval_jaxpr/vmap(jvp(bij,bjk->bik))/dot_general | solution.py:53
  173.9 2.2 %bitcast_select_fusion.2 = f32[4,32,32,32]{3,2,0,1:T(8,128)S(1)} fusion(f32[32,32,4,32]{3,1,2,0:T(8,128)S(1)} %fusion.184, f32[4,32,32]{2,0,1:T(4,128)S(1)} %get-tuple-element.743, f32[32,32]{1,0:T(8,128)S(1)} %get-tuple-element.744, f32[32,32]{1,0:T(8,128)S(1)} %get-tuple-element.745, f32[4,32,32]{2,0,1:T(4,128)S(1)} %get-tuple-element.746, ...), kind=kOutput, calls=%fused_computation.99.clone.1 | convolution fusion | flops 50921472 | bytes 1093920 | tf_op jit(solution)/shard_map/while/body/eval_jaxpr/vmap(jvp(bik,blk->bil))/dot_general | solution.py:54
  179.4 2.3 %fusion.187 = f32[4,4,4,32]{1,2,3,0:T(4,128)S(1)} fusion(f32[4,4,4,32]{1,2,3,0:T(4,128)S(1)} %get-tuple-element.787, s32[]{:T(128)} %get-tuple-element.785, f32[4,32,1024]{2,0,1:T(4,128)S(1)} %reshape.2358, f32[32]{0:T(128)S(1)} %get-tuple-element.747, f32[32,1024]{1,0:T(8,128)S(1)} %mul.2955, f32[4]{0:T(128)S(1)} %get-tuple-element.748, ...), kind=kOutput, calls=%fused_computation.113.clone.1 | convolution fusion | flops 6685184 | bytes 722436 | tf_op jit(solution)/shard_map/while/body/eval_jaxpr/pbq,rbq->prb/dot_general | solution.py:71
  186.5 2.9 %fusion.184 = f32[32,32,4,32]{3,1,2,0:T(8,128)S(1)} fusion(f32[32,32,32]{2,1,0:T(8,128)S(1)} %get-tuple-element.723, f32[4,32]{0,1:T(8,128)S(1)} %copy.83, f32[32,32,32]{2,1,0:T(8,128)S(1)} %get-tuple-element.731, f32[32]{0:T(128)S(1)} %bitcast.320, f32[4]{0:T(128)S(1)} %get-tuple-element.732, f32[32,32,32]{2,1,0:T(8,128)S(1)} %get-tuple-element.733, ...), kind=kOutput, calls=%fused_computation.100.clone.1 | convolution fusion | flops 51576832 | bytes 955408 | tf_op jit(solution)/shard_map/while/body/eval_jaxpr/vmap(jvp(bij,bjk->bik))/dot_general | solution.py:53
  190.1 2.2 %bitcast_select_fusion.2 = f32[4,32,32,32]{3,2,0,1:T(8,128)S(1)} fusion(f32[32,32,4,32]{3,1,2,0:T(8,128)S(1)} %fusion.184, f32[4,32,32]{2,0,1:T(4,128)S(1)} %get-tuple-element.743, f32[32,32]{1,0:T(8,128)S(1)} %get-tuple-element.744, f32[32,32]{1,0:T(8,128)S(1)} %get-tuple-element.745, f32[4,32,32]{2,0,1:T(4,128)S(1)} %get-tuple-element.746, ...), kind=kOutput, calls=%fused_computation.99.clone.1 | convolution fusion | flops 50921472 | bytes 1093920 | tf_op jit(solution)/shard_map/while/body/eval_jaxpr/vmap(jvp(bik,blk->bil))/dot_general | solution.py:54
  195.7 2.3 %fusion.187 = f32[4,4,4,32]{1,2,3,0:T(4,128)S(1)} fusion(f32[4,4,4,32]{1,2,3,0:T(4,128)S(1)} %get-tuple-element.787, s32[]{:T(128)} %get-tuple-element.785, f32[4,32,1024]{2,0,1:T(4,128)S(1)} %reshape.2358, f32[32]{0:T(128)S(1)} %get-tuple-element.747, f32[32,1024]{1,0:T(8,128)S(1)} %mul.2955, f32[4]{0:T(128)S(1)} %get-tuple-element.748, ...), kind=kOutput, calls=%fused_computation.113.clone.1 | convolution fusion | flops 6685184 | bytes 722436 | tf_op jit(solution)/shard_map/while/body/eval_jaxpr/pbq,rbq->prb/dot_general | solution.py:71
  (272 shorter events, 77.1 us)
Async XLA Ops:
  4.2 37.6 %all-to-all-start = ((s32[64,4,1]{1,2,0:T(1,128)}), s32[64,4,1]{1,2,0:T(1,128)S(1)}, u32[]{:S(2)}, u32[]{:S(2)}) async-start(s32[64,4,1]{1,2,0:T(1,128)} %bitcast.49), calls=%async_computation | async-start | bytes 65536 | tf_op jit(solution)/shard_map/all_to_all | solution.py:172
  40.5 14.2 %copy-start.2 = (f32[32]{0:T(128)S(1)}, f32[32]{0:T(128)}, u32[]{:S(2)}) copy-start(f32[32]{0:T(128)} %param.19) | copy-start | bytes 388
  41.8 48.8 %copy-start = (f32[32,1024]{1,0:T(8,128)S(1)}, f32[32,1024]{1,0:T(8,128)}, u32[]{:S(2)}) copy-start(f32[32,1024]{1,0:T(8,128)} %param.18) | copy-start | bytes 393220
  41.8 42.0 %all-to-all-start.1 = ((f32[64,4,1024]{2,1,0:T(4,128)}), f32[64,4,1024]{2,1,0:T(4,128)S(1)}, u32[]{:S(2)}, u32[]{:S(2)}) async-start(f32[64,4,1024]{2,1,0:T(4,128)} %all_to_all.32), calls=%async_computation.1 | async-start | bytes 2097152 | tf_op jit(solution)/shard_map/all_to_all | solution.py:171
  83.8 18.5 %all-to-all-start.3 = ((f32[64,4,1]{1,2,0:T(1,128)}), f32[64,4,1]{1,2,0:T(1,128)S(1)}, u32[]{:S(2)}, u32[]{:S(2)}) async-start(f32[64,4,1]{1,2,0:T(1,128)} %bitcast.55), calls=%async_computation.3 | async-start | bytes 65536 | tf_op jit(solution)/shard_map/all_to_all | solution.py:177
  102.3 32.5 %all-to-all-start.2 = ((f32[64,4,1024]{2,1,0:T(4,128)}), f32[64,4,1024]{2,1,0:T(4,128)S(1)}, u32[]{:S(2)}, u32[]{:S(2)}) async-start(f32[64,4,1024]{2,1,0:T(4,128)} %all_to_all.35), calls=%async_computation.2 | async-start | bytes 2097152 | tf_op jit(solution)/shard_map/all_to_all | solution.py:176
  109.6 3.2 %collective-permute-start = (f32[]{:T(128)}, f32[]{:T(128)}, u32[]{:S(2)}, u32[]{:S(2)}) collective-permute-start(f32[]{:T(128)} %get-tuple-element.534), channel_id=1, source_target_pairs={{0,1},{1,0},{2,3},{3,2},{4,5},{5,4},{6,7},{7,6},{8,9},{9,8},{10,11... | collective-permute-start | bytes 20 | tf_op jit(solution)/shard_map/ppermute | solution.py:184
  114.1 5.4 %collective-permute-start.1 = (f32[]{:T(128)}, f32[]{:T(128)}, u32[]{:S(2)}, u32[]{:S(2)}) collective-permute-start(f32[]{:T(128)} %add.943), channel_id=1, source_target_pairs={{0,2},{1,3},{2,0},{3,1},{4,6},{5,7},{6,4},{7,5},{8,10},{9,11},{10,... | collective-permute-start | bytes 20 | tf_op jit(solution)/shard_map/ppermute | solution.py:184
  120.1 6.9 %collective-permute-start.2 = (f32[]{:T(128)}, f32[]{:T(128)}, u32[]{:S(2)}, u32[]{:S(2)}) collective-permute-start(f32[]{:T(128)} %add.944), channel_id=1, source_target_pairs={{0,4},{1,5},{2,6},{3,7},{4,0},{5,1},{6,2},{7,3},{8,12},{9,13},{10,... | collective-permute-start | bytes 20 | tf_op jit(solution)/shard_map/ppermute | solution.py:184
  135.9 68.4 %copy-start.1 = (f32[4,128]{1,0:T(4,128)S(1)}, f32[4,128]{1,0:T(4,128)}, u32[]{:S(2)}) copy-start(f32[4,128]{1,0:T(4,128)} %param.12) | copy-start | bytes 6148
